TPU v7x, 32 devices: a whole 2x2x4 slice. The times are simulated.
32 devices in a mesh: row: 4 (over z), col: 4 (over x, core), tm: 2 (over y).
Axes of the slice: x: 2, y: 2, z: 4, core: 2. Of those that a mesh axis runs over, the one named last changes fastest.
Arguments:
- samples: bfloat16 [1024, 4, 2, 16384], P('row', None, 'tm', 'col'), may hold values from -6 to 6
- whitening: bfloat16 [1024, 1024], replicated, may hold values from -0.1875 to 0.1875
- ridge: float32 [2048], P('col'), may hold values from 2 to 20
- slab_start: int32 [1], replicated, may hold values from 0 to 63
- panels: int32 [4], replicated, may hold values from 0 to 3, as said below
Outputs:
- trailing: float32 [131072, 2048], P(('row', 'tm'), 'col')
- factor: bfloat16 [2, 131072, 512], P(None, ('row', 'tm'))
Inputs may be any that keep to these rules, and one draw needn't show every extreme that they name: `panels`: each panel index once.
All inputs are finite; a program needn't handle non-finite values.
Results may differ from a plain program's by a relative error of at most 0.012.
The roundings to bfloat16 on the way count: a program that leaves them out, or rounds other values in their place, can miss the bound.
Values may be sent and summed in bfloat16 or wider, within the bound.
A program may use at most 256 MiB of HBM per device.

v0:
```python
import jax
import jax.numpy as jnp
from jax import lax
from jax.sharding import PartitionSpec as P

S = 1024
PANEL = 512
PANELS = 2


def broadcast(block, axis, holder):
    block = jnp.where(lax.axis_index(axis) == holder, block, jnp.zeros_like(block))
    return lax.psum(block, axis)


def on_device(samples, whitening, ridge, slab_start, panels):
    moved = lax.all_to_all(samples, "row", split_axis=1, concat_axis=0, tiled=True)
    local_width = moved.shape[3]
    series = moved.reshape(moved.shape[0], local_width)
    whitened = jnp.dot(whitening, series, preferred_element_type=jnp.float32).astype(jnp.bfloat16)
    col_count = lax.axis_size("col")
    tm_count = lax.axis_size("tm")
    rows_here = col_count * local_width
    slab_width = PANEL * col_count
    scale = S ** (-0.5)
    slab_first = slab_start[0] * slab_width
    owner_index = slab_first // rows_here
    slab_offset = slab_first % rows_here
    col_index = lax.axis_index("col")
    self_index = lax.axis_index("row") * tm_count + lax.axis_index("tm")
    row_series = lax.all_gather(whitened, "col", axis=1, tiled=True)
    piece = lax.dynamic_slice_in_dim(row_series, slab_offset + col_index * PANEL, PANEL, 1)
    slab_part = broadcast(piece, ("row", "tm"), owner_index)
    covariance = (
        lax.dot_general(
            row_series, slab_part, (((0,), (0,)), ((), ())), preferred_element_type=jnp.float32
        )
        * scale
    )
    owner_flag = (self_index == owner_index).astype(jnp.float32)
    ridge_rows = slab_offset + col_index * PANEL
    zero_index = jnp.zeros((), jnp.int32)
    diag_block = (
        lax.dynamic_slice(covariance, (ridge_rows, zero_index), (PANEL, PANEL))
        + jnp.diag(ridge) * owner_flag
    )
    covariance = lax.dynamic_update_slice(covariance, diag_block, (ridge_rows, zero_index))
    identity = jnp.eye(PANEL, dtype=jnp.float32)
    factors = []
    finished = col_index < 0
    for section in range(PANELS):
        panel_index = panels[section]
        finished = finished | (col_index == panel_index)
        pivot_local = lax.dynamic_slice_in_dim(
            covariance, slab_offset + panel_index * PANEL, PANEL, 0
        )
        pivot_rows = broadcast(pivot_local, ("row", "tm"), owner_index)
        pivot_safe = jnp.where(col_index == panel_index, pivot_rows, identity)
        lower_factor = jnp.linalg.cholesky(pivot_safe)
        panel_now = jax.scipy.linalg.solve_triangular(lower_factor, covariance.T, lower=True).T
        small_block = lower_factor
        panel_bf = broadcast(panel_now.astype(jnp.bfloat16), "col", panel_index)
        small_block = broadcast(small_block, "col", panel_index)
        coupling = jax.scipy.linalg.solve_triangular(small_block, pivot_rows, lower=True).T
        coupling_bf = coupling.astype(jnp.bfloat16)
        covariance = covariance - lax.dot_general(
            panel_bf, coupling_bf, (((1,), (1,)), ((), ())), preferred_element_type=jnp.float32
        )
        factors.append(panel_bf)
    trailing = jnp.where(finished, jnp.zeros_like(covariance), covariance)
    return (trailing, jnp.stack(factors))


def solution(mesh):
    in_specs = (P("row", None, "tm", "col"), P(), P("col"), P(), P())
    out_specs = (P(("row", "tm"), "col"), P(None, ("row", "tm"), None))
    return jax.shard_map(
        on_device, mesh=mesh, in_specs=in_specs, out_specs=out_specs, check_vma=False
    )
```

profile of v0, /device:TPU:0, one launch (start us, length us, event | category | flops | bytes accessed | tf_op | source)
XLA Modules:
  0.0 1940.5 jit_solution(8248852513893661534)
XLA Ops:
  7.2 11.5 copy.58
  18.7 189.4 %all_to_all.15 = bf16[256,4,1,4096]{3,0,2,1:T(8,128)(2,1)S(1)} all-to-all(bf16[256,4,1,4096]{3,0,2,1:T(8,128)(2,1)} %copy.58), channel_id=1, replica_groups=mesh['row'=4,'col'=4,'tm'=2] {'row'}, dimensions={1} | all-to-all | bytes 16777216 | tf_op jit(solution)/shard_map/all_to_all | solution.py:17
  208.1 10.8 convolution_convert_fusion
  219.7 200.6 %all-gather.2.cloned.1.call-done = bf16[1024,16384]{1,0:T(8,128)(2,1)} async-done(((bf16[1024,4096]{1,0:T(8,128)(2,1)}), bf16[1024,16384]{1,0:T(8,128)(2,1)}) %all-gather.2.cloned.1.call-update) | async-done | bytes 33554448 | tf_op jit(solution)/shard_map/all_gather | solution.py:31
  424.6 78.0 %all-reduce.9.cloned.1.call-done = bf16[1024,512]{1,0:T(8,128)(2,1)} async-done(((bf16[1024,512]{1,0:T(8,128)(2,1)}), bf16[1024,512]{1,0:T(8,128)(2,1)}) %all-reduce.9.cloned.1.call-update) | async-done | bytes 1048592 | tf_op jit(solution)/shard_map/psum | solution.py:13
  502.6 31.8 %convolution_multiply_fusion = f32[16384,512]{0,1:T(8,128)} fusion(bf16[1024,16384]{1,0:T(8,128)(2,1)} %all-gather.2.cloned.1.call-done, bf16[1024,512]{1,0:T(8,128)(2,1)} %all-reduce.9.cloned.1.call-done), kind=kOutput, calls=%fused_computation.12 | convolution fusion | flops 17188257792 | bytes 68157440 | tf_op jit(solution)/shard_map/dot_general | solution.py:35
  545.4 77.0 %all-reduce.11.cloned.1.call-done = f32[512,512]{0,1:T(8,128)} async-done(((f32[512,512]{0,1:T(8,128)}), f32[512,512]{0,1:T(8,128)}) %all-reduce.11.cloned.1.call-update) | async-done | bytes 1048592 | tf_op jit(solution)/shard_map/psum | solution.py:13
  623.1 11.7 cholesky.286
  635.0 9.8 custom-call.31
  645.6 11.7 cholesky.305
  657.4 10.2 custom-call.32
  668.8 11.7 cholesky.326
  680.7 9.8 custom-call.33
  691.3 11.9 cholesky.343
  717.8 39.3 %custom-call.34 = f32[4,128,128]{1,2,0:T(8,128)S(1)} custom-call(f32[4,128,128]{2,1,0:T(8,128)S(1)} %get-tuple-element.33), custom_call_target="InvertDiagBlocksLowerTriangular" | custom-call | tf_op jit(solution)/shard_map/jit(_solve_triangular)/triangular_solve | solution.py:60
  757.2 9.7 fusion.30
  767.0 12.8 convolution_subtract_fusion.4
  789.3 16.7 convolution_subtract_fusion.3
  806.0 11.7 fusion.96
  817.7 22.9 %fusion.15 = f32[128,16384]{1,0:T(8,128)} fusion(f32[128,16384]{1,0:T(8,128)} %fusion.96, f32[128,16384]{1,0:T(8,128)} %fusion.98, f32[128,16384]{1,0:T(8,128)} %copy-done.2, f32[512,16384]{1,0:T(8,128)} %bitcast.173, f32[512,512]{0,1:T(8,128)S(1)} %get-tuple-element.357), kind=kOutput, calls=%fused_computation.31 | convolution fusion | flops 9678356480 | bytes 42139648 | tf_op jit(solution)/shard_map/jit(_solve_triangular)/triangular_solve | solution.py:60
  840.6 11.2 fusion.95
  851.8 17.2 fusion.21
  879.6 39.3 %custom-call.35 = f32[4,128,128]{1,2,0:T(8,128)S(1)} custom-call(f32[4,128,128]{2,1,0:T(8,128)S(1)} %get-tuple-element.34), custom_call_target="InvertDiagBlocksLowerTriangular" | custom-call | tf_op jit(solution)/shard_map/jit(_solve_triangular)/triangular_solve | solution.py:64
  923.8 234.4 %all-reduce.13.cloned.1.call-done = bf16[16384,512]{0,1:T(8,128)(2,1)} async-done(((bf16[16384,512]{0,1:T(8,128)(2,1)}), bf16[16384,512]{0,1:T(8,128)(2,1)}) %all-reduce.13.cloned.1.call-update) | async-done | bytes 16777232 | tf_op jit(solution)/shard_map/psum | solution.py:13
  1158.2 28.8 %convolution_subtract_fusion = f32[16384,512]{0,1:T(8,128)} fusion(f32[16384,512]{0,1:T(8,128)} %dynamic_update_slice.3, bf16[16384,512]{0,1:T(8,128)(2,1)} %all-reduce.13.cloned.1.call-done, bf16[128,512]{1,0:T(8,128)(2,1)S(1)} %fusion.91, f32[128,512]{1,0:T(8,128)S(1)} %fusion.92, f32[128,512]{1,0:T(8,128)S(1)} %fusion.94, f32[128,512]{1,0:T(8,128)S(1)} %fusion.60), kind=kOutput, calls=%fused_computation.25 | convolution fusion | flops 8600420352 | bytes 84803584 | tf_op jit(solution)/shard_map/dot_general | solution.py:66
  1190.5 77.5 %all-reduce.17.cloned.1.call-done = f32[512,512]{0,1:T(8,128)} async-done(((f32[512,512]{0,1:T(8,128)}), f32[512,512]{0,1:T(8,128)}) %all-reduce.17.cloned.1.call-update) | async-done | bytes 1048592 | tf_op jit(solution)/shard_map/psum | solution.py:13
  1268.7 11.7 cholesky.358
  1280.6 9.8 custom-call.36
  1291.2 11.7 cholesky.377
  1303.0 10.3 custom-call.37
  1314.4 11.7 cholesky.398
  1326.3 9.8 custom-call.38
  1336.9 11.8 cholesky.415
  1363.9 39.3 %custom-call.39 = f32[4,128,128]{1,2,0:T(8,128)S(1)} custom-call(f32[4,128,128]{2,1,0:T(8,128)S(1)} %get-tuple-element.35), custom_call_target="InvertDiagBlocksLowerTriangular" | custom-call | tf_op jit(solution)/shard_map/jit(_solve_triangular)/triangular_solve | solution.py:60
  1403.3 9.8 fusion.28
  1413.1 12.8 convolution_subtract_fusion.2
  1425.9 9.5 fusion.88
  1435.4 16.6 convolution_subtract_fusion.1
  1452.0 11.7 fusion.86
  1463.7 22.9 %fusion.12 = f32[128,16384]{1,0:T(8,128)} fusion(f32[128,16384]{1,0:T(8,128)} %fusion.86, f32[128,16384]{1,0:T(8,128)} %fusion.88, f32[128,16384]{1,0:T(8,128)} %copy-done.3, f32[512,16384]{1,0:T(8,128)} %bitcast.169, f32[512,512]{0,1:T(8,128)S(1)} %get-tuple-element.358), kind=kOutput, calls=%fused_computation.30 | convolution fusion | flops 9678356480 | bytes 42139648 | tf_op jit(solution)/shard_map/jit(_solve_triangular)/triangular_solve | solution.py:60
  1486.6 11.2 fusion.85
  1497.8 17.2 fusion.19
  1524.7 39.5 %custom-call.40 = f32[4,128,128]{1,2,0:T(8,128)S(1)} custom-call(f32[4,128,128]{2,1,0:T(8,128)S(1)} %get-tuple-element.36), custom_call_target="InvertDiagBlocksLowerTriangular" | custom-call | tf_op jit(solution)/shard_map/jit(_solve_triangular)/triangular_solve | solution.py:64
  1569.0 234.4 %all-reduce.19.cloned.1.call-done = bf16[16384,512]{0,1:T(8,128)(2,1)} async-done(((bf16[16384,512]{0,1:T(8,128)(2,1)}), bf16[16384,512]{0,1:T(8,128)(2,1)}) %all-reduce.19.cloned.1.call-update) | async-done | bytes 16777232 | tf_op jit(solution)/shard_map/psum | solution.py:13
  1803.4 29.5 %subtract_select_fusion = f32[16384,512]{0,1:T(8,128)} fusion(f32[16384,512]{0,1:T(8,128)} %convolution_subtract_fusion, bf16[16384,512]{0,1:T(8,128)(2,1)} %all-reduce.19.cloned.1.call-done, pred[]{:T(512)S(6)} %or.26, bf16[128,512]{1,0:T(8,128)(2,1)S(1)} %fusion.81, f32[128,512]{1,0:T(8,128)S(1)} %fusion.82, f32[128,512]{1,0:T(8,128)S(1)} %fusion.84, ...), kind=kOutput, calls=%fused_computation.11 | convolution fusion | flops 8608808960 | bytes 84803584 | tf_op jit(solution)/shard_map/dot_general | solution.py:66
  1832.9 33.4 %copy.88 = f32[16384,512]{1,0:T(8,128)} copy(f32[16384,512]{0,1:T(8,128)} %subtract_select_fusion) | data formatting | bytes 67108864
  1866.3 23.0 %pad_maximum_fusion = bf16[2,16384,512]{1,2,0:T(8,128)(2,1)} fusion(bf16[1,16384,512]{1,2,0:T(8,128)(2,1)} %bitcast.175, bf16[1,16384,512]{1,2,0:T(8,128)(2,1)} %bitcast.174), kind=kLoop, calls=%fused_computation.10 | loop fusion | flops 16777216 | bytes 67108864 | tf_op jit(solution)/shard_map/stack | solution.py:71
  1889.3 44.1 %copy.89 = bf16[2,16384,512]{2,1,0:T(8,128)(2,1)} copy(bf16[2,16384,512]{1,2,0:T(8,128)(2,1)} %pad_maximum_fusion) | data formatting | bytes 67108864
  (208 shorter events, 121.2 us)
Async XLA Ops:
  7.2 200.9 %copy-start = (bf16[1024,1024]{1,0:T(8,128)(2,1)S(1)}, bf16[1024,1024]{1,0:T(8,128)(2,1)}, u32[]{:S(2)}) copy-start(bf16[1024,1024]{1,0:T(8,128)(2,1)} %param.11) | copy-start | bytes 6291460
  7.2 413.1 %all-gather.2.cloned.1.call-start = ((), (), s32[]{:S(2)}) async-start(), calls=%async_computation.1 | async-start | bytes 41943040 | tf_op jit(solution)/shard_map/all_gather | solution.py:31
  218.9 204.5 %copy-start.7 = (s32[4]{0:T(128)S(1)}, s32[4]{0:T(128)}, u32[]{:S(2)}) copy-start(s32[4]{0:T(128)} %param.14) | copy-start | bytes 52
  218.9 283.7 %all-reduce.9.cloned.1.call-start = ((), (), s32[]{:S(2)}) async-start(), calls=%async_computation.2 | async-start | bytes 2097152 | tf_op jit(solution)/shard_map/psum | solution.py:13
  423.1 199.3 %all-reduce.11.cloned.1.call-start = ((), (), s32[]{:S(2)}) async-start(), calls=%async_computation.3 | async-start | bytes 2097152 | tf_op jit(solution)/shard_map/psum | solution.py:13
  424.6 109.7 %copy-start.6 = (f32[512]{0:T(512)S(1)}, f32[512]{0:T(512)}, u32[]{:S(2)}) copy-start(f32[512]{0:T(512)} %param.12) | copy-start | bytes 6148
  544.5 325.2 %all-reduce.15.cloned.1.call-start = ((), (), s32[]{:S(2)}) async-start(), calls=%async_computation.5 | async-start | bytes 2097152 | tf_op jit(solution)/shard_map/psum | solution.py:13
  757.2 401.0 %all-reduce.13.cloned.1.call-start = ((), (), s32[]{:S(2)}) async-start(), calls=%async_computation.4 | async-start | bytes 33554432 | tf_op jit(solution)/shard_map/psum | solution.py:13
  767.0 12.8 copy-start.2
  868.9 50.0 %copy-start.4 = (f32[512,512]{0,1:T(8,128)S(1)}, f32[512,512]{0,1:T(8,128)}, u32[]{:S(2)}) copy-start(f32[512,512]{0,1:T(8,128)} %all-reduce.11.cloned.1.call-done) | copy-start | bytes 3145732
  869.0 399.0 %all-reduce.17.cloned.1.call-start = ((), (), s32[]{:S(2)}) async-start(), calls=%async_computation.6 | async-start | bytes 2097152 | tf_op jit(solution)/shard_map/psum | solution.py:13
  1189.6 325.4 %all-reduce.21.cloned.1.call-start = ((), (), s32[]{:S(2)}) async-start(), calls=%async_computation.8 | async-start | bytes 2097152 | tf_op jit(solution)/shard_map/psum | solution.py:13
  1403.2 400.1 %all-reduce.19.cloned.1.call-start = ((), (), s32[]{:S(2)}) async-start(), calls=%async_computation.7 | async-start | bytes 33554432 | tf_op jit(solution)/shard_map/psum | solution.py:13
  1413.0 12.8 copy-start.3
  1515.0 49.2 %copy-start.5 = (f32[512,512]{0,1:T(8,128)S(1)}, f32[512,512]{0,1:T(8,128)}, u32[]{:S(2)}) copy-start(f32[512,512]{0,1:T(8,128)} %all-reduce.17.cloned.1.call-done) | copy-start | bytes 3145732
  1889.3 44.1 %copy-start.1 = (bf16[1024,1024]{1,0:T(8,128)(2,1)S(1)}, bf16[1024,1024]{1,0:T(8,128)(2,1)}, u32[]{:S(2)}) copy-start(bf16[1024,1024]{1,0:T(8,128)(2,1)} %param.11) | copy-start | bytes 6291460
Sparse Core Ops, SparseCore 0:
  219.0 201.1 all-gather.1
  424.3 78.2 all-reduce.8
  544.6 77.7 all-reduce.10
  757.3 37.1 all-reduce.14
  869.1 289.0 all-reduce.12
  1189.7 78.1 all-reduce.16
  1403.4 36.2 all-reduce.20
  1515.1 288.2 all-reduce.18
where the time goes:
time: 1950 us; the launch traced here: 1940 us
  waiting for transfers between devices  902 us (46%)
  other arithmetic  389 us (20%)
  matrix products  304 us (16%)
  blocking collectives  189 us (10%)
  local copies, waits for them, and re-layouts  131 us (7%)
  between operations  23.4 us (1%)
    psum x7, waiting for transfers between devices, broadcast(): return lax.psum(block, axis)  701 us
    all_gather x1, waiting for transfers between devices, on_device(): row_series = lax.all_gather(whitened, 'col', axis=1, tiled=True)  201 us
    all_to_all x1, blocking collectives, on_device(): lax.all_to_all(samples, 'row', split_axis=1, concat_axis=0, tiled=True)  189 us
    another operation x14, matrix products, on_device(): jax.scipy.linalg.solve_triangular(lower_factor, covariance.T, lower=True)  189 us
    another operation x29, other arithmetic, on_device(): lower_factor = jnp.linalg.cholesky(pivot_safe)  159 us
    unnamed x19, local copies, waits for them, and re-layouts  89.1 us
    another operation x4, other arithmetic, on_device(): jax.scipy.linalg.solve_triangular(small_block, pivot_rows, lower=True)  81.5 us
    another operation x3, other arithmetic, on_device(): jax.scipy.linalg.solve_triangular(lower_factor, covariance.T, lower=True)  78.6 us
  transfers between devices with their start and end apart: 8, of which 6 were waited for; matrix products, arithmetic and copies ran while one was open for 17% of the time, Pallas kernels for 0%

commit v1 on v0

--- a/solution.py
+++ b/solution.py
@@ -10,7 +10,11 @@
 
 def broadcast(block, axis, holder):
     block = jnp.where(lax.axis_index(axis) == holder, block, jnp.zeros_like(block))
-    return lax.psum(block, axis)
+
+    def review_ports(row_data):
+        return lax.all_gather(row_data, axis).sum(axis=0)
+
+    return review_ports(block)
 
 
 def on_device(samples, whitening, ridge, slab_start, panels):

time: 1950 us -> 2680 us (1.37)
  waiting for transfers between devices: 902 us -> 1220 us
  other arithmetic: 389 us -> 593 us
  local copies, waits for them, and re-layouts: 131 us -> 335 us
    all_gather x0 -> x7, waiting for transfers between devices: none -> 1020 us  [review_ports(): return lax.all_gather(row_data, axis).sum(axis=0)]
    psum x7 -> x0, waiting for transfers between devices: 701 us -> none  [broadcast(): return lax.psum(block, axis)]
    reduce_sum x0 -> x7, other arithmetic: none -> 207 us  [review_ports(): return lax.all_gather(row_data, axis).sum(axis=0)]
    all_gather x0 -> x4, local copies, waits for them, and re-layouts: none -> 181 us  [review_ports(): return lax.all_gather(row_data, axis).sum(axis=0)]
    unnamed x19 -> x21, local copies, waits for them, and re-layouts: 89.1 us -> 112 us
  transfers between devices with their start and end apart: 8 -> 8, of which waited for: 6 -> 6; matrix products, arithmetic and copies ran while one was open for 17% -> 13% of each run, Pallas kernels for 0% -> 0%
where the time goes in v1:
time: 2680 us; the launch traced here: 2670 us
  waiting for transfers between devices  1220 us (46%)
  other arithmetic  593 us (22%)
  local copies, waits for them, and re-layouts  335 us (12%)
  matrix products  307 us (11%)
  blocking collectives  189 us (7%)
    all_gather x7, waiting for transfers between devices, review_ports(): return lax.all_gather(row_data, axis).sum(axis=0)  1020 us
    reduce_sum x7, other arithmetic, review_ports(): return lax.all_gather(row_data, axis).sum(axis=0)  207 us
    all_gather x1, waiting for transfers between devices, on_device(): row_series = lax.all_gather(whitened, 'col', axis=1, tiled=True)  201 us
    all_to_all x1, blocking collectives, on_device(): lax.all_to_all(samples, 'row', split_axis=1, concat_axis=0, tiled=True)  189 us
    another operation x14, matrix products, on_device(): jax.scipy.linalg.solve_triangular(lower_factor, covariance.T, lower=True)  188 us
    all_gather x4, local copies, waits for them, and re-layouts, review_ports(): return lax.all_gather(row_data, axis).sum(axis=0)  181 us
    another operation x29, other arithmetic, on_device(): lower_factor = jnp.linalg.cholesky(pivot_safe)  158 us
    unnamed x21, local copies, waits for them, and re-layouts  112 us
  transfers between devices with their start and end apart: 8, of which 6 were waited for; matrix products, arithmetic and copies ran while one was open for 13% of the time, Pallas kernels for 0%

profile of v1, /device:TPU:0, one launch (start us, length us, event | category | flops | bytes accessed | tf_op | source)
XLA Modules:
  0.0 2668.6 jit_solution(18134837151229665901)
XLA Ops:
  7.2 11.5 copy.52
  18.7 189.4 %all_to_all.15 = bf16[256,4,1,4096]{3,0,2,1:T(8,128)(2,1)S(1)} all-to-all(bf16[256,4,1,4096]{3,0,2,1:T(8,128)(2,1)} %copy.52), channel_id=1, replica_groups=mesh['row'=4,'col'=4,'tm'=2] {'row'}, dimensions={1} | all-to-all | bytes 16777216 | tf_op jit(solution)/shard_map/all_to_all | solution.py:21
  208.1 10.8 convolution_convert_fusion
  219.7 200.6 %all-gather.16.cloned.1.call-done = bf16[1024,16384]{1,0:T(8,128)(2,1)} async-done(((bf16[1024,4096]{1,0:T(8,128)(2,1)}), bf16[1024,16384]{1,0:T(8,128)(2,1)}) %all-gather.16.cloned.1.call-update) | async-done | bytes 33554448 | tf_op jit(solution)/shard_map/all_gather | solution.py:35
  424.6 123.2 %all-gather.18.cloned.1.call-done = bf16[8192,512]{1,0:T(8,128)(2,1)} async-done(((bf16[1024,512]{1,0:T(8,128)(2,1)}), bf16[8192,512]{1,0:T(8,128)(2,1)}) %all-gather.18.cloned.1.call-update) | async-done | bytes 8388624 | tf_op jit(solution)/shard_map/all_gather | solution.py:15
  553.0 31.5 %convolution_multiply_fusion = f32[16384,512]{0,1:T(8,128)} fusion(bf16[1024,16384]{1,0:T(8,128)(2,1)} %all-gather.16.cloned.1.call-done, bf16[1024,512]{1,0:T(8,128)(2,1)S(1)} %reduce_sum.72), kind=kOutput, calls=%fused_computation.12 | convolution fusion | flops 17188257792 | bytes 68157440 | tf_op jit(solution)/shard_map/dot_general | solution.py:39
  595.5 122.0 %all-gather.20.cloned.1.call-done = f32[4096,512]{0,1:T(8,128)} async-done(((f32[512,512]{0,1:T(8,128)}), f32[4096,512]{0,1:T(8,128)}) %all-gather.20.cloned.1.call-update) | async-done | bytes 8388624 | tf_op jit(solution)/shard_map/all_gather | solution.py:15
  717.5 11.5 copy.101
  733.2 11.7 cholesky.286
  745.0 9.8 custom-call.31
  755.6 11.8 cholesky.305
  779.4 11.7 cholesky.326
  791.3 9.8 custom-call.33
  802.7 12.1 cholesky.343
  829.8 39.3 %custom-call.34 = f32[4,128,128]{1,2,0:T(8,128)S(1)} custom-call(f32[4,128,128]{2,1,0:T(8,128)S(1)} %get-tuple-element.33), custom_call_target="InvertDiagBlocksLowerTriangular" | custom-call | tf_op jit(solution)/shard_map/jit(_solve_triangular)/triangular_solve | solution.py:64
  878.9 12.8 convolution_subtract_fusion.4
  901.2 16.5 convolution_subtract_fusion.3
  917.8 11.7 fusion.96
  929.5 22.7 fusion.15
  952.2 11.2 fusion.95
  963.4 17.2 fusion.21
  1003.1 39.3 %custom-call.35 = f32[4,128,128]{1,2,0:T(8,128)S(1)} custom-call(f32[4,128,128]{2,1,0:T(8,128)S(1)} %get-tuple-element.34), custom_call_target="InvertDiagBlocksLowerTriangular" | custom-call | tf_op jit(solution)/shard_map/jit(_solve_triangular)/triangular_solve | solution.py:68
  1047.2 324.4 %all-gather.22.cloned.1.call-done = bf16[65536,512]{0,1:T(8,128)(2,1)} async-done(((bf16[16384,512]{0,1:T(8,128)(2,1)}), bf16[65536,512]{0,1:T(8,128)(2,1)}) %all-gather.22.cloned.1.call-update) | async-done | bytes 67108880 | tf_op jit(solution)/shard_map/all_gather | solution.py:15
  1371.6 83.6 %reshape.97 = bf16[4,16384,512]{1,0,2:T(4,128)(2,1)} reshape(bf16[65536,512]{0,1:T(8,128)(2,1)} %all-gather.22.cloned.1.call-done) | data formatting | bytes 134217728 | tf_op jit(solution)/shard_map/all_gather | solution.py:15
  1455.3 91.2 %reduce_sum.74 = bf16[16384,512]{0,1:T(8,128)(2,1)} reduce(bf16[4,16384,512]{1,0,2:T(4,128)(2,1)} %reshape.97, bf16[]{:T(256)} %constant.169.clone.1), dimensions={0}, to_apply=%region_10.13 | reduce | flops 25165824 | bytes 83886080 | tf_op jit(solution)/shard_map/reduce_sum | solution.py:15
  1546.4 28.8 %convolution_subtract_fusion = f32[16384,512]{0,1:T(8,128)} fusion(f32[16384,512]{0,1:T(8,128)} %dynamic_update_slice.3, bf16[16384,512]{0,1:T(8,128)(2,1)} %reduce_sum.74, bf16[128,512]{1,0:T(8,128)(2,1)S(1)} %fusion.91, f32[128,512]{1,0:T(8,128)S(1)} %fusion.92, f32[128,512]{1,0:T(8,128)S(1)} %fusion.94, f32[128,512]{1,0:T(8,128)S(1)} %fusion.60), kind=kOutput, calls=%fused_computation.25 | convolution fusion | flops 8600420352 | bytes 84803584 | tf_op jit(solution)/shard_map/dot_general | solution.py:70
  1578.8 123.7 %all-gather.26.cloned.1.call-done = f32[4096,512]{0,1:T(8,128)} async-done(((f32[512,512]{0,1:T(8,128)}), f32[4096,512]{0,1:T(8,128)}) %all-gather.26.cloned.1.call-update) | async-done | bytes 8388624 | tf_op jit(solution)/shard_map/all_gather | solution.py:15
  1702.5 11.5 copy.102
  1718.2 11.7 cholesky.358
  1730.1 9.8 custom-call.36
  1740.7 11.8 cholesky.377
  1764.5 11.7 cholesky.398
  1787.8 12.1 cholesky.415
  1814.8 39.3 %custom-call.39 = f32[4,128,128]{1,2,0:T(8,128)S(1)} custom-call(f32[4,128,128]{2,1,0:T(8,128)S(1)} %get-tuple-element.35), custom_call_target="InvertDiagBlocksLowerTriangular" | custom-call | tf_op jit(solution)/shard_map/jit(_solve_triangular)/triangular_solve | solution.py:64
  1864.0 12.8 convolution_subtract_fusion.2
  1886.3 16.5 convolution_subtract_fusion.1
  1902.8 11.7 fusion.86
  1914.5 22.7 fusion.12
  1937.2 11.2 fusion.85
  1948.5 17.2 fusion.19
  1987.4 39.3 %custom-call.40 = f32[4,128,128]{1,2,0:T(8,128)S(1)} custom-call(f32[4,128,128]{2,1,0:T(8,128)S(1)} %get-tuple-element.36), custom_call_target="InvertDiagBlocksLowerTriangular" | custom-call | tf_op jit(solution)/shard_map/jit(_solve_triangular)/triangular_solve | solution.py:68
  2031.5 325.2 %all-gather.28.cloned.1.call-done = bf16[65536,512]{0,1:T(8,128)(2,1)} async-done(((bf16[16384,512]{0,1:T(8,128)(2,1)}), bf16[65536,512]{0,1:T(8,128)(2,1)}) %all-gather.28.cloned.1.call-update) | async-done | bytes 67108880 | tf_op jit(solution)/shard_map/all_gather | solution.py:15
  2356.7 83.6 %reshape.100 = bf16[4,16384,512]{1,0,2:T(4,128)(2,1)} reshape(bf16[65536,512]{0,1:T(8,128)(2,1)} %all-gather.28.cloned.1.call-done) | data formatting | bytes 134217728 | tf_op jit(solution)/shard_map/all_gather | solution.py:15
  2440.3 91.2 %reduce_sum.77 = bf16[16384,512]{0,1:T(8,128)(2,1)} reduce(bf16[4,16384,512]{1,0,2:T(4,128)(2,1)} %reshape.100, bf16[]{:T(256)} %constant.169.clone.1), dimensions={0}, to_apply=%region_13.17 | reduce | flops 25165824 | bytes 83886080 | tf_op jit(solution)/shard_map/reduce_sum | solution.py:15
  2531.5 29.5 %subtract_select_fusion = f32[16384,512]{0,1:T(8,128)} fusion(f32[16384,512]{0,1:T(8,128)} %convolution_subtract_fusion, bf16[16384,512]{0,1:T(8,128)(2,1)} %reduce_sum.77, pred[]{:T(512)S(6)} %or.26, bf16[128,512]{1,0:T(8,128)(2,1)S(1)} %fusion.81, f32[128,512]{1,0:T(8,128)S(1)} %fusion.82, f32[128,512]{1,0:T(8,128)S(1)} %fusion.84, f32[128,512]{1,0:T(8,128)S(1)} %fusion.57), kind=kOutput, calls=%fused_computation.11 | convolution fusion | flops 8608808960 | bytes 84803584 | tf_op jit(solution)/shard_map/dot_general | solution.py:70
  2561.0 33.4 %copy.82 = f32[16384,512]{1,0:T(8,128)} copy(f32[16384,512]{0,1:T(8,128)} %subtract_select_fusion) | data formatting | bytes 67108864
  2594.5 23.0 pad_maximum_fusion
  2617.5 44.1 %copy.83 = bf16[2,16384,512]{2,1,0:T(8,128)(2,1)} copy(bf16[2,16384,512]{1,2,0:T(8,128)(2,1)} %pad_maximum_fusion) | data formatting | bytes 67108864
  (221 shorter events, 220.0 us)
Async XLA Ops:
  7.2 200.9 %copy-start = (bf16[1024,1024]{1,0:T(8,128)(2,1)S(1)}, bf16[1024,1024]{1,0:T(8,128)(2,1)}, u32[]{:S(2)}) copy-start(bf16[1024,1024]{1,0:T(8,128)(2,1)} %param.11) | copy-start | bytes 6291460
  7.2 413.1 %all-gather.16.cloned.1.call-start = ((), (), s32[]{:S(2)}) async-start(), calls=%async_computation.1 | async-start | bytes 41943040 | tf_op jit(solution)/shard_map/all_gather | solution.py:35
  218.9 204.5 %copy-start.7 = (s32[4]{0:T(128)S(1)}, s32[4]{0:T(128)}, u32[]{:S(2)}) copy-start(s32[4]{0:T(128)} %param.14) | copy-start | bytes 52
  218.9 328.8 %all-gather.18.cloned.1.call-start = ((), (), s32[]{:S(2)}) async-start(), calls=%async_computation.2 | async-start | bytes 9437184 | tf_op jit(solution)/shard_map/all_gather | solution.py:15
  423.1 294.3 %all-gather.20.cloned.1.call-start = ((), (), s32[]{:S(2)}) async-start(), calls=%async_computation.3 | async-start | bytes 9437184 | tf_op jit(solution)/shard_map/all_gather | solution.py:15
  553.0 31.6 %copy-start.6 = (f32[512]{0:T(512)S(1)}, f32[512]{0:T(512)}, u32[]{:S(2)}) copy-start(f32[512]{0:T(512)} %param.12) | copy-start | bytes 6148
  594.7 386.7 %all-gather.24.cloned.1.call-start = ((), (), s32[]{:S(2)}) async-start(), calls=%async_computation.5 | async-start | bytes 5242880 | tf_op jit(solution)/shard_map/all_gather | solution.py:15
  733.1 34.5 %copy-start.4 = (f32[512,512]{1,0:T(8,128)}, f32[512,512]{1,0:T(8,128)S(1)}, u32[]{:S(2)}) copy-start(f32[512,512]{1,0:T(8,128)S(1)} %fusion.33) | copy-start | bytes 3145732
  869.1 502.5 %all-gather.22.cloned.1.call-start = ((), (), s32[]{:S(2)}) async-start(), calls=%async_computation.4 | async-start | bytes 83886080 | tf_op jit(solution)/shard_map/all_gather | solution.py:15
  878.9 12.8 copy-start.2
  980.6 721.9 %all-gather.26.cloned.1.call-start = ((), (), s32[]{:S(2)}) async-start(), calls=%async_computation.6 | async-start | bytes 9437184 | tf_op jit(solution)/shard_map/all_gather | solution.py:15
  1577.9 387.8 %all-gather.30.cloned.1.call-start = ((), (), s32[]{:S(2)}) async-start(), calls=%async_computation.8 | async-start | bytes 5242880 | tf_op jit(solution)/shard_map/all_gather | solution.py:15
  1718.2 34.5 %copy-start.5 = (f32[512,512]{1,0:T(8,128)}, f32[512,512]{1,0:T(8,128)S(1)}, u32[]{:S(2)}) copy-start(f32[512,512]{1,0:T(8,128)S(1)} %fusion.32) | copy-start | bytes 3145732
  1854.2 502.6 %all-gather.28.cloned.1.call-start = ((), (), s32[]{:S(2)}) async-start(), calls=%async_computation.7 | async-start | bytes 83886080 | tf_op jit(solution)/shard_map/all_gather | solution.py:15
  1864.0 12.8 copy-start.3
  2617.4 44.1 %copy-start.1 = (bf16[1024,1024]{1,0:T(8,128)(2,1)S(1)}, bf16[1024,1024]{1,0:T(8,128)(2,1)}, u32[]{:S(2)}) copy-start(bf16[1024,1024]{1,0:T(8,128)(2,1)} %param.11) | copy-start | bytes 6291460
Sparse Core Ops, SparseCore 0:
  219.0 201.1 all-gather.15
  423.2 124.4 all-gather.17
  594.8 122.6 all-gather.19
  869.2 32.6 all-gather.23
  980.7 390.9 all-gather.21
  1578.0 124.4 all-gather.25
  1854.3 32.6 all-gather.29
  1965.8 390.9 all-gather.27
